TPU v7x, 32 devices: a whole 2x2x4 slice. The times are simulated.
32 devices in a mesh: grp: 2 (over x), row: 16 (over z, y, core).
Axes of the slice: x: 2, y: 2, z: 4, core: 2. Of those that a mesh axis runs over, the one named last changes fastest.
Arguments:
- inputs: bfloat16 [8192, 8192], P(('grp', 'row')), parts along dimension 0, may hold values from -6 to 6
- out_grads: bfloat16 [8192, 8192], P(('grp', 'row')), parts along dimension 0, may hold values from -6 to 6
- proj_in: bfloat16 [8192, 64], replicated, may hold values from -0.0625 to 0.0625
- proj_out: bfloat16 [8192, 64], replicated, may hold values from -0.0625 to 0.0625
- example_ids: int32 [8192], P(('grp', 'row')), parts along dimension 0, may hold values from 0 to 7, as said below
Outputs:
- gram: float32 [256, 128], P(('grp', 'row')), parts along dimension 0
There are 2 independent parts, one for each index of `grp`. A program takes and returns all parts, laid end to end along the dimension named above; an argument that names none is the same for every part. Nothing has to cross between parts.
Inputs may be any that keep to these rules, and one draw needn't show every extreme that they name: `example_ids`: within each aligned block of 256 tokens every value 0 to 7 appears exactly 32 times, in an order drawn from the seed.
All inputs are finite; a program needn't handle non-finite values.
Results may differ from a plain program's by a relative error of at most 0.0025.
Values may be sent and summed in bfloat16 or wider, within the bound.
No kernel may reach another device: no remote copies, remote signals or barrier semaphores. Data moves between devices by JAX's collectives and lax.ppermute only.
A program may use at most 64 MiB of HBM per device.

v0:
```python
import math

import jax
import jax.numpy as jnp
from jax import lax
from jax.sharding import PartitionSpec as P

RANK = 64
TPE = 32
EX_DEV = 8


def tile_of(mine, other):
    product = lax.dot_general(
        mine, other, (((1,), (1,)), ((), ())), preferred_element_type=jnp.float32
    )
    return product / RANK


def shards(inputs, out_grads, proj_in, proj_out, example_ids):
    xproj = jnp.dot(inputs, proj_in, preferred_element_type=jnp.float32).astype(jnp.bfloat16)
    gproj = jnp.dot(out_grads, proj_out, preferred_element_type=jnp.float32).astype(jnp.bfloat16)
    onehot = (example_ids[None, :] == jnp.arange(EX_DEV, dtype=jnp.int32)[:, None]).astype(
        jnp.bfloat16
    )
    weighted = onehot[:, :, None] * gproj[None, :, :]
    outer = jnp.einsum("etp,tq->epq", weighted, xproj, preferred_element_type=jnp.float32)
    scale_factor = 1.0 / math.sqrt(TPE)
    features = (outer.reshape(EX_DEV, RANK * RANK) * scale_factor).astype(jnp.bfloat16)
    return tile_of(features, lax.all_gather(features, "row", axis=0, tiled=True))


def solution(mesh):
    in_specs = (P(("grp", "row"), None), P(("grp", "row"), None), P(), P(), P(("grp", "row")))
    out_specs = P(("grp", "row"), None)
    return jax.shard_map(shards, mesh=mesh, in_specs=in_specs, out_specs=out_specs, check_vma=False)
```

profile of v0, /device:TPU:0, one launch (start us, length us, event | category | flops | bytes accessed | tf_op | source)
XLA Modules:
  0.0 65.8 jit_solution(11964064832021179859)
XLA Ops:
  6.5 0.0 copy-start
  6.5 0.0 all-gather.2.cloned.1.call-start
  6.5 0.8 %fusion.5 = bf16[8,256]{1,0:T(8,128)(2,1)S(1)} fusion(s32[256]{0:T(256)} %param.9), kind=kLoop, calls=%fused_computation.10 | loop fusion | flops 4096 | bytes 5120 | tf_op jit(solution)/shard_map/convert_element_type | solution.py:23
  7.3 3.9 %convolution_convert_fusion.1 = bf16[256,64]{0,1:T(8,128)(2,1)S(1)} fusion(bf16[256,8192]{1,0:T(8,128)(2,1)} %param.6, bf16[8192,64]{0,1:T(8,128)(2,1)} %param.8), kind=kOutput, calls=%fused_computation.3 | convolution fusion | flops 268451840 | bytes 5275648 | tf_op jit(solution)/shard_map/dot_general | solution.py:22
  11.2 0.0 copy-done
  11.2 3.9 %fusion = bf16[8,64,64]{2,1,0:T(8,128)(2,1)S(1)} fusion(bf16[256,8192]{1,0:T(8,128)(2,1)} %param.5, bf16[8192,64]{0,1:T(8,128)(2,1)S(1)} %copy-done, bf16[256,64]{0,1:T(8,128)(2,1)S(1)} %convolution_convert_fusion.1, bf16[8,256]{1,0:T(8,128)(2,1)S(1)} %fusion.5), kind=kOutput, calls=%fused_computation.1 | convolution fusion | flops 285425664 | bytes 5345280 | tf_op jit(solution)/shard_map/etp,tq->epq/dot_general | solution.py:27
  15.1 0.8 %convert_element_type.23 = bf16[8,4096]{1,0:T(8,128)(2,1)} reshape(bf16[8,64,64]{2,1,0:T(8,128)(2,1)S(1)} %fusion) | data formatting | bytes 131072 | tf_op jit(solution)/shard_map/convert_element_type | solution.py:29
  15.9 0.0 all-gather.2.cloned.1.call-update
  15.9 40.7 %all-gather.2.cloned.1.call-done = bf16[128,4096]{1,0:T(8,128)(2,1)} async-done(((bf16[8,4096]{1,0:T(8,128)(2,1)}), bf16[128,4096]{1,0:T(8,128)(2,1)}) %all-gather.2.cloned.1.call-update) | async-done | bytes 1048592 | tf_op jit(solution)/shard_map/all_gather | solution.py:30
  56.7 2.2 %convolution_multiply_fusion.1 = f32[8,128]{1,0:T(8,128)} fusion(bf16[8,4096]{1,0:T(8,128)(2,1)} %convert_element_type.23, bf16[128,4096]{1,0:T(8,128)(2,1)} %all-gather.2.cloned.1.call-done), kind=kOutput, calls=%fused_computation.5 | convolution fusion | flops 8389632 | bytes 1118208 | tf_op jit(solution)/shard_map/dot_general | solution.py:14
Async XLA Ops:
  6.5 4.7 %copy-start = (bf16[8192,64]{0,1:T(8,128)(2,1)S(1)}, bf16[8192,64]{0,1:T(8,128)(2,1)}, u32[]{:S(2)}) copy-start(bf16[8192,64]{0,1:T(8,128)(2,1)} %param.7) | copy-start | bytes 3145732
  6.5 50.1 %all-gather.2.cloned.1.call-start = ((), (), s32[]{:S(2)}) async-start(), calls=%async_computation | async-start | bytes 1114112 | tf_op jit(solution)/shard_map/all_gather | solution.py:30
Sparse Core Ops, SparseCore 0:
  16.0 40.5 all-gather.1
where the time goes:
time: 65.9 us; the launch traced here: 65.8 us
  waiting for transfers between devices  40.8 us (62%)
  between operations  13.4 us (20%)
  matrix products  10 us (15%)
  local copies, waits for them, and re-layouts  0.8 us (1%)
  other arithmetic  0.77 us (1%)
    all_gather x1, waiting for transfers between devices, shards(): lax.all_gather(features, 'row', axis=0, tiled=True)  40.7 us
    dot_general x1, matrix products, shards(): jnp.einsum('etp,tq->epq', weighted, xproj, preferred_element_type=jnp.flo...  3.89 us
    dot_general x1, matrix products, shards(): jnp.dot(out_grads, proj_out, preferred_element_type=jnp.float32)  3.88 us
    dot_general x1, matrix products, tile_of(): lax.dot_general(mine, other, (((1,), (1,)), ((), ())), preferred_element_...  2.24 us
  transfers between devices with their start and end apart: 1, of which 1 were waited for; matrix products, arithmetic and copies ran while one was open for 0% of the time, Pallas kernels for 0%

commit v1 on v0

v1 whole, which is shorter than its diff:
```python
import functools
import math

import jax
import jax.numpy as jnp
from jax import lax
from jax.experimental import pallas as pl
from jax.experimental.pallas import tpu as pltpu
from jax.sharding import PartitionSpec as P

RANK = 64
TPE = 32
EX_DEV = 8
CHUNKS = 4
PACK = 16
LANES = 128
NT = (((1,), (1,)), ((), ()))
VM = pl.BlockSpec(memory_space=pltpu.VMEM)
ANY = pl.BlockSpec(memory_space=pl.ANY)


def features_kernel(ids_ref, x_hbm, g_hbm, pi_hbm, po_hbm, f_ref, xv, gv, piv, pov, ax, ag, sems):
    tokens, depth = x_hbm.shape
    rank = pi_hbm.shape[0]
    half = rank // 2
    step = depth // CHUNKS
    sides = ((x_hbm, pi_hbm, xv, piv, ax), (g_hbm, po_hbm, gv, pov, ag))

    def copies(side, c):
        act_hbm, proj_hbm, act, proj, _ = sides[side]
        cols = pl.ds(pl.multiple_of(c * step, step), step)
        return (
            pltpu.make_async_copy(proj_hbm.at[:, cols], proj.at[:, cols], sems.at[2 * side, c]),
            pltpu.make_async_copy(act_hbm.at[:, cols], act.at[:, cols], sems.at[2 * side + 1, c]),
        )

    for side in (0, 1):
        for c in range(CHUNKS):
            for copy in copies(side, c):
                copy.start()
    ax[...] = jnp.zeros_like(ax)
    ag[...] = jnp.zeros_like(ag)
    for side in (0, 1):
        _, _, act, proj, acc = sides[side]

        @pl.loop(0, CHUNKS)
        def _(c, side=side, act=act, proj=proj, acc=acc):
            for copy in copies(side, c):
                copy.wait()
            cols = pl.ds(pl.multiple_of(c * step, step), step)
            acc[...] += lax.dot_general(
                proj[:, cols], act[:, cols], NT, preferred_element_type=jnp.float32
            )

    gt = ag[...].astype(jnp.bfloat16).astype(jnp.float32)
    xt = ax[...].astype(jnp.bfloat16)
    mask = ids_ref[...] == lax.broadcasted_iota(jnp.int32, (EX_DEV, tokens), 0)
    mask = mask.astype(jnp.float32)
    rows = [
        jnp.concatenate([gt[p : p + 1] * mask, gt[p + half : p + half + 1] * mask], axis=1)
        for p in range(half)
    ]
    left = jnp.concatenate(rows, axis=0).astype(jnp.bfloat16)
    zero = jnp.zeros_like(xt)
    right = jnp.concatenate(
        [jnp.concatenate([xt, zero], axis=1), jnp.concatenate([zero, xt], axis=1)], axis=0
    )
    outer = lax.dot_general(left, right, NT, preferred_element_type=jnp.float32)
    f_ref[...] = (outer * (1.0 / math.sqrt(TPE))).astype(jnp.bfloat16).reshape(f_ref.shape)


def features_of(inputs, out_grads, proj_in, proj_out, example_ids):
    tokens, depth = inputs.shape
    rank = proj_in.shape[1]
    return pl.pallas_call(
        features_kernel,
        out_shape=pltpu.VMEM((rank * EX_DEV // 2 // PACK, PACK, 2 * rank), jnp.bfloat16),
        in_specs=[VM, ANY, ANY, ANY, ANY],
        out_specs=VM,
        scratch_shapes=[
            pltpu.VMEM((tokens, depth), jnp.bfloat16),
            pltpu.VMEM((tokens, depth), jnp.bfloat16),
            pltpu.VMEM((rank, depth), jnp.bfloat16),
            pltpu.VMEM((rank, depth), jnp.bfloat16),
            pltpu.VMEM((rank, tokens), jnp.float32),
            pltpu.VMEM((rank, tokens), jnp.float32),
            pltpu.SemaphoreType.DMA((4, CHUNKS)),
        ],
        name="features",
    )(example_ids.reshape(1, tokens), inputs, out_grads, proj_in.T, proj_out.T)


def near(x):
    return pltpu.with_memory_space_constraint(x, pltpu.VMEM)


def gram_kernel(f_ref, fp_ref, cols_ref, *refs):
    before, after = refs[: len(refs) - 2], refs[len(refs) - 2 :]
    chunks, width, _ = cols_ref.shape
    acc = jnp.zeros((2 * PACK, width), jnp.float32)
    for q in range(0, chunks, 2):
        left = jnp.concatenate(
            [
                jnp.concatenate([f_ref[q], f_ref[q + 1]], axis=1),
                jnp.concatenate([fp_ref[q], fp_ref[q + 1]], axis=1),
            ],
            axis=0,
        )
        right = jnp.concatenate([cols_ref[q], cols_ref[q + 1]], axis=1)
        acc += lax.dot_general(left, right, NT, preferred_element_type=jnp.float32)
    for side in (0, 1):
        even = acc[side * PACK : side * PACK + EX_DEV]
        odd = acc[side * PACK + EX_DEV : (side + 1) * PACK]
        odd = jnp.concatenate([odd[:, EX_DEV:], odd[:, :EX_DEV]], axis=1)
        both = (even + odd) * (1.0 / RANK)
        if before:
            both = jnp.concatenate([before[side][...], both], axis=1)
        after[side][...] = both


def gram_of(f, fp, cols, before=()):
    chunks, width, lanes = cols.shape
    n_cols = width + (before[0].shape[1] if before else 0)
    return pl.pallas_call(
        gram_kernel,
        out_shape=[pltpu.VMEM((EX_DEV, n_cols), jnp.float32)] * 2,
        in_specs=[VM] * (3 + len(before)),
        out_specs=[VM, VM],
        cost_estimate=pl.CostEstimate(
            flops=4 * PACK * width * chunks * lanes,
            bytes_accessed=2 * chunks * lanes * (width + 2 * PACK),
            transcendentals=0,
        ),
        name="gram",
    )(*map(near, (f, fp, cols, *before)))


def place_kernel(orders, own_ref, other_ref, out_ref):
    me = lax.axis_index("row")
    width, n_cols = own_ref.shape[1], out_ref.shape[1]
    col = lax.broadcasted_iota(jnp.int32, (width, n_cols), 1)
    row = lax.broadcasted_iota(jnp.int32, (width, n_cols), 0)
    offset = (col // EX_DEV) ^ me

    def source(core):
        pos = jnp.zeros_like(col)
        for j, (bit0, bit1) in enumerate(zip(*orders)):
            bit = jnp.where(core == 0, bit0, bit1)
            pos += jnp.where((offset & bit) != 0, 1 << j, 0)
        return pos * PACK + col % EX_DEV

    core = me & 1
    mine = (offset & 1) == 0
    pick_own = (mine & (row == source(core))).astype(jnp.float32)
    pick_other = (~mine & (row == source(1 - core))).astype(jnp.float32)
    dot = functools.partial(
        jnp.dot, precision=lax.Precision.HIGHEST, preferred_element_type=jnp.float32
    )
    out_ref[...] = dot(own_ref[...], pick_own) + dot(other_ref[...], pick_other)


def shards(n, inputs, out_grads, proj_in, proj_out, example_ids):
    bits = [1 << b for b in range(n.bit_length() - 2, 0, -1)]
    orders = (bits, bits[:-2] + bits[-2:][::-1])
    core = [(i, i ^ 1) for i in range(n)]
    f = features_of(inputs, out_grads, proj_in, proj_out, example_ids)
    fp = lax.ppermute(f, "row", core)
    held = f
    for j in range(len(bits)):
        perm = [(i, i ^ orders[i & 1][j]) for i in range(n)]
        came = lax.ppermute(held, "row", perm)
        if j < len(bits) - 1:
            held = jnp.concatenate([held, came], axis=1)
    own, other = gram_of(f, fp, came, gram_of(f, fp, held))
    got = lax.ppermute(other, "row", core)
    return pl.pallas_call(
        functools.partial(place_kernel, orders),
        out_shape=jax.ShapeDtypeStruct((EX_DEV, n * EX_DEV), jnp.float32),
        in_specs=[VM, VM],
        out_specs=VM,
        name="place",
    )(near(own), near(got))


def solution(mesh):
    in_specs = (P(("grp", "row"), None), P(("grp", "row"), None), P(), P(), P(("grp", "row")))
    out_specs = P(("grp", "row"), None)
    body = functools.partial(shards, mesh.shape["row"])
    return jax.shard_map(body, mesh=mesh, in_specs=in_specs, out_specs=out_specs, check_vma=False)
```

time: 65.9 us -> 27.8 us (0.42)
  waiting for transfers between devices: 40.8 us -> 13.5 us
  between operations: 13.4 us -> 0.03 us
  matrix products: 10 us -> 0 us
  Pallas kernels: 0 us -> 7.32 us
  starting transfers between devices: 0.01 us -> 6.77 us
  local copies, waits for them, and re-layouts: 0.8 us -> 0 us
  other arithmetic: 0.77 us -> 0.03 us
    all_gather x1 -> x0, waiting for transfers between devices: 40.7 us -> none  [shards(): lax.all_gather(features, 'row', axis=0, tiled=True)]
    ppermute x0 -> x5, waiting for transfers between devices: none -> 13.5 us  [the longest x3 11.1 us: shards(): came = lax.ppermute(held, 'row', perm)]
    dot_general x3 -> x0, matrix products: 10 us -> none  [the longest x1 3.89 us: shards(): jnp.einsum('etp,tq->epq', weighted, xproj, preferred_element_type=jnp.flo...]
    pallas_call x0 -> x4, Pallas kernels: none -> 7.32 us  [the longest x1 5.91 us: features_of(): pl.pallas_call(features_kernel, out_shape=pltpu.VMEM((rank * EX_DEV // 2...]
    ppermute x0 -> x5, starting transfers between devices: none -> 6.77 us  [the longest x3 6.76 us: shards(): came = lax.ppermute(held, 'row', perm)]
    convert_element_type x1 -> x0, local copies, waits for them, and re-layouts: 0.79 us -> none  [shards(): (outer.reshape(EX_DEV, RANK * RANK) * scale_factor).astype(jnp.bfloat16)]
    convert_element_type x1 -> x0, other arithmetic: 0.77 us -> none  [shards(): (example_ids[None, :] == jnp.arange(EX_DEV, dtype=jnp.int32)[:, None]).as...]
  transfers between devices with their start and end apart: 1 -> 5, of which waited for: 1 -> 5; matrix products, arithmetic and copies ran while one was open for 0% -> 0% of each run, Pallas kernels for 0% -> 1%
where the time goes in v1:
time: 27.8 us; the launch traced here: 27.6 us
  waiting for transfers between devices  13.5 us (49%)
  Pallas kernels  7.32 us (26%)
  starting transfers between devices  6.77 us (24%)
    ppermute x3, waiting for transfers between devices, shards(): came = lax.ppermute(held, 'row', perm)  11.1 us
    ppermute x3, starting transfers between devices, shards(): came = lax.ppermute(held, 'row', perm)  6.76 us
    pallas_call x1, Pallas kernels, features_of(): pl.pallas_call(features_kernel, out_shape=pltpu.VMEM((rank * EX_DEV // 2...  5.91 us
    ppermute x1, waiting for transfers between devices, shards(): fp = lax.ppermute(f, 'row', core)  1.25 us
    ppermute x1, waiting for transfers between devices, shards(): got = lax.ppermute(other, 'row', core)  1.18 us
    pallas_call x1, Pallas kernels, shards(): pl.pallas_call(functools.partial(place_kernel, orders), out_shape=jax.Sha...  0.83 us
    pallas_call x2, Pallas kernels, gram_of(): pl.pallas_call(gram_kernel, out_shape=[pltpu.VMEM((EX_DEV, n_cols), jnp.f...  0.58 us
  transfers between devices with their start and end apart: 5, of which 5 were waited for; matrix products, arithmetic and copies ran while one was open for 0% of the time, Pallas kernels for 1%

profile of v1, /device:TPU:0, one launch (start us, length us, event | category | flops | bytes accessed | tf_op | source)
XLA Modules:
  0.0 27.6 jit_solution(39956381578024482)
XLA Ops:
  0.0 5.9 %features.1.f_ref = bf16[16,16,128]{2,1,0:T(8,128)(2,1)S(1)} custom-call(s32[1,256]{1,0:T(1,128)} %bitcast.5, bf16[256,8192]{1,0:T(8,128)(2,1)} %x_hbm.1, bf16[256,8192]{1,0:T(8,128)(2,1)} %g_hbm.1, bf16[64,8192]{1,0:T(8,128)(2,1)} %bitcast.3, bf16[64,8192]{1,0:T(8,128)(2,1)} %bitcast.4), custom_call_target="tpu_custom_call" | custom-call | tf_op jit(solution)/shard_map/features/pallas_call | solution.py:75
  5.9 4.1 %collective-permute-start.1 = (bf16[16,16,128]{2,1,0:T(8,128)(2,1)S(1)}, bf16[16,16,128]{2,1,0:T(8,128)(2,1)S(1)}, u32[]{:S(2)}, u32[]{:S(2)}) collective-permute-start(bf16[16,16,128]{2,1,0:T(8,128)(2,1)S(1)} %features.1.f_ref), channel_id=1, source_target_pairs={{0,8},{1,9},{2,10},{3,11},{4,12},{5,13},{6,14},{7,15},{8,0},{9,1},... | collective-permute-start | bytes 196616 | tf_op jit(solution)/shard_map/ppermute | solution.py:171
  10.1 3.6 %collective-permute-done.1 = bf16[16,16,128]{2,1,0:T(8,128)(2,1)S(1)} collective-permute-done((bf16[16,16,128]{2,1,0:T(8,128)(2,1)S(1)}, bf16[16,16,128]{2,1,0:T(8,128)(2,1)S(1)}, u32[]{:S(2)}, u32[]{:S(2)}) %collective-permute-start.1) | collective-permute-done | bytes 65568 | tf_op jit(solution)/shard_map/ppermute | solution.py:171
  13.7 0.6 %collective-permute-start.2 = (bf16[16,32,128]{2,1,0:T(8,128)(2,1)S(1)}, bf16[16,32,128]{2,1,0:T(8,128)(2,1)S(1)}, u32[]{:S(2)}, u32[]{:S(2)}) collective-permute-start(bf16[16,32,128]{2,1,0:T(8,128)(2,1)S(1)} %pad_maximum_fusion.1), channel_id=1, source_target_pairs={{0,4},{1,3},{2,6},{3,1},{4,0},{5,7},{6,2},{7,5},{8,12},{9,11},{10,... | collective-permute-start | bytes 393224 | tf_op jit(solution)/shard_map/ppermute | solution.py:171
  14.3 4.5 %collective-permute-done.2 = bf16[16,32,128]{2,1,0:T(8,128)(2,1)S(1)} collective-permute-done((bf16[16,32,128]{2,1,0:T(8,128)(2,1)S(1)}, bf16[16,32,128]{2,1,0:T(8,128)(2,1)S(1)}, u32[]{:S(2)}, u32[]{:S(2)}) %collective-permute-start.2) | collective-permute-done | bytes 131104 | tf_op jit(solution)/shard_map/ppermute | solution.py:171
  18.9 2.0 %collective-permute-start.3 = (bf16[16,64,128]{2,1,0:T(8,128)(2,1)S(1)}, bf16[16,64,128]{2,1,0:T(8,128)(2,1)S(1)}, u32[]{:S(2)}, u32[]{:S(2)}) collective-permute-start(bf16[16,64,128]{2,1,0:T(8,128)(2,1)S(1)} %pad_maximum_fusion.cols_ref), channel_id=1, source_target_pairs={{0,2},{1,5},{2,0},{3,7},{4,6},{5,1},{6,4},{7,3},{8,10},{9,13},{10,... | collective-permute-start | bytes 786440 | tf_op jit(solution)/shard_map/ppermute | solution.py:171
  20.9 0.0 collective-permute-start
  20.9 1.3 %collective-permute-done.fp_ref = bf16[16,16,128]{2,1,0:T(8,128)(2,1)S(1)} collective-permute-done((bf16[16,16,128]{2,1,0:T(8,128)(2,1)S(1)}, bf16[16,16,128]{2,1,0:T(8,128)(2,1)S(1)}, u32[]{:S(2)}, u32[]{:S(2)}) %collective-permute-start) | collective-permute-done | bytes 65568 | tf_op jit(solution)/shard_map/ppermute | solution.py:167
  22.1 0.3 gram.2
  22.4 2.9 %collective-permute-done.3.cols_ref = bf16[16,64,128]{2,1,0:T(8,128)(2,1)S(1)} collective-permute-done((bf16[16,64,128]{2,1,0:T(8,128)(2,1)S(1)}, bf16[16,64,128]{2,1,0:T(8,128)(2,1)S(1)}, u32[]{:S(2)}, u32[]{:S(2)}) %collective-permute-start.3) | collective-permute-done | bytes 262176 | tf_op jit(solution)/shard_map/ppermute | solution.py:171
  25.3 0.3 %gram.3 = (f32[8,128]{1,0:T(8,128)S(1)}, f32[8,128]{1,0:T(8,128)S(1)}) custom-call(bf16[16,16,128]{2,1,0:T(8,128)(2,1)S(1)} %features.1.f_ref, bf16[16,16,128]{2,1,0:T(8,128)(2,1)S(1)} %collective-permute-done.fp_ref, bf16[16,64,128]{2,1,0:T(8,128)(2,1)S(1)} %collective-permute-done.3.cols_ref, f32[8,64]{1,0:T(8,128)S(1)} %get-tuple-element.9.refs_0_, ...), custom_call_target="tpu_custom_call" | custom-call | flops 8388608 | bytes 393216 | tf_op jit(solution)/shard_map/gram/pallas_call | solution.py:124
  25.6 0.0 collective-permute-start.4
  25.6 1.2 %collective-permute-done.4.other_ref = f32[8,128]{1,0:T(8,128)S(1)} collective-permute-done((f32[8,128]{1,0:T(8,128)S(1)}, f32[8,128]{1,0:T(8,128)S(1)}, u32[]{:S(2)}, u32[]{:S(2)}) %collective-permute-start.4) | collective-permute-done | bytes 4128 | tf_op jit(solution)/shard_map/ppermute | solution.py:175
  26.8 0.8 %place.1 = f32[8,128]{1,0:T(8,128)} custom-call(f32[8,128]{1,0:T(8,128)S(1)} %get-tuple-element.11.own_ref, f32[8,128]{1,0:T(8,128)S(1)} %collective-permute-done.4.other_ref), custom_call_target="tpu_custom_call" | custom-call | tf_op jit(solution)/shard_map/place/pallas_call | solution.py:176
  (2 shorter events, 0.0 us)
Async XLA Ops:
  5.9 7.8 %collective-permute-start.1 = (bf16[16,16,128]{2,1,0:T(8,128)(2,1)S(1)}, bf16[16,16,128]{2,1,0:T(8,128)(2,1)S(1)}, u32[]{:S(2)}, u32[]{:S(2)}) collective-permute-start(bf16[16,16,128]{2,1,0:T(8,128)(2,1)S(1)} %features.1.f_ref), channel_id=1, source_target_pairs={{0,8},{1,9},{2,10},{3,11},{4,12},{5,13},{6,14},{7,15},{8,0},{9,1},... | collective-permute-start | bytes 196616 | tf_op jit(solution)/shard_map/ppermute | solution.py:171
  13.7 5.1 %collective-permute-start.2 = (bf16[16,32,128]{2,1,0:T(8,128)(2,1)S(1)}, bf16[16,32,128]{2,1,0:T(8,128)(2,1)S(1)}, u32[]{:S(2)}, u32[]{:S(2)}) collective-permute-start(bf16[16,32,128]{2,1,0:T(8,128)(2,1)S(1)} %pad_maximum_fusion.1), channel_id=1, source_target_pairs={{0,4},{1,3},{2,6},{3,1},{4,0},{5,7},{6,2},{7,5},{8,12},{9,11},{10,... | collective-permute-start | bytes 393224 | tf_op jit(solution)/shard_map/ppermute | solution.py:171
  18.9 6.4 %collective-permute-start.3 = (bf16[16,64,128]{2,1,0:T(8,128)(2,1)S(1)}, bf16[16,64,128]{2,1,0:T(8,128)(2,1)S(1)}, u32[]{:S(2)}, u32[]{:S(2)}) collective-permute-start(bf16[16,64,128]{2,1,0:T(8,128)(2,1)S(1)} %pad_maximum_fusion.cols_ref), channel_id=1, source_target_pairs={{0,2},{1,5},{2,0},{3,7},{4,6},{5,1},{6,4},{7,3},{8,10},{9,13},{10,... | collective-permute-start | bytes 786440 | tf_op jit(solution)/shard_map/ppermute | solution.py:171
  20.9 1.3 %collective-permute-start = (bf16[16,16,128]{2,1,0:T(8,128)(2,1)S(1)}, bf16[16,16,128]{2,1,0:T(8,128)(2,1)S(1)}, u32[]{:S(2)}, u32[]{:S(2)}) collective-permute-start(bf16[16,16,128]{2,1,0:T(8,128)(2,1)S(1)} %features.1.f_ref), channel_id=1, source_target_pairs={{0,1},{1,0},{2,3},{3,2},{4,5},{5,4},{6,7},{7,6},{8,9},{9,8},{10,11... | collective-permute-start | bytes 196616 | tf_op jit(solution)/shard_map/ppermute | solution.py:167
  25.6 1.2 %collective-permute-start.4 = (f32[8,128]{1,0:T(8,128)S(1)}, f32[8,128]{1,0:T(8,128)S(1)}, u32[]{:S(2)}, u32[]{:S(2)}) collective-permute-start(f32[8,128]{1,0:T(8,128)S(1)} %get-tuple-element.12), channel_id=1, source_target_pairs={{0,1},{1,0},{2,3},{3,2},{4,5},{5,4},{6,7},{7,6},{8,9},{9,8},{10,11... | collective-permute-start | bytes 12296 | tf_op jit(solution)/shard_map/ppermute | solution.py:175

commit v2 on v1

--- a/solution.py
+++ b/solution.py
@@ -94,19 +94,17 @@
     return pltpu.with_memory_space_constraint(x, pltpu.VMEM)
 
 
-def gram_kernel(f_ref, fp_ref, cols_ref, *refs):
-    before, after = refs[: len(refs) - 2], refs[len(refs) - 2 :]
-    chunks, width, _ = cols_ref.shape
-    acc = jnp.zeros((2 * PACK, width), jnp.float32)
+def gram_kernel(n_cols, f_ref, fp_ref, *refs):
+    cols, before, after = refs[:n_cols], refs[n_cols:-2], refs[-2:]
+    chunks = f_ref.shape[0]
+
+    def wide(ref, q):
+        return jnp.concatenate([ref[q], ref[q + 1]], axis=1)
+
+    acc = jnp.zeros((2 * PACK, sum(ref.shape[1] for ref in cols)), jnp.float32)
     for q in range(0, chunks, 2):
-        left = jnp.concatenate(
-            [
-                jnp.concatenate([f_ref[q], f_ref[q + 1]], axis=1),
-                jnp.concatenate([fp_ref[q], fp_ref[q + 1]], axis=1),
-            ],
-            axis=0,
-        )
-        right = jnp.concatenate([cols_ref[q], cols_ref[q + 1]], axis=1)
+        left = jnp.concatenate([wide(f_ref, q), wide(fp_ref, q)], axis=0)
+        right = jnp.concatenate([wide(ref, q) for ref in cols], axis=0)
         acc += lax.dot_general(left, right, NT, preferred_element_type=jnp.float32)
     for side in (0, 1):
         even = acc[side * PACK : side * PACK + EX_DEV]
@@ -119,12 +117,13 @@
 
 
 def gram_of(f, fp, cols, before=()):
-    chunks, width, lanes = cols.shape
+    chunks, _, lanes = f.shape
+    width = sum(c.shape[1] for c in cols)
     n_cols = width + (before[0].shape[1] if before else 0)
     return pl.pallas_call(
-        gram_kernel,
+        functools.partial(gram_kernel, len(cols)),
         out_shape=[pltpu.VMEM((EX_DEV, n_cols), jnp.float32)] * 2,
-        in_specs=[VM] * (3 + len(before)),
+        in_specs=[VM] * (2 + len(cols) + len(before)),
         out_specs=[VM, VM],
         cost_estimate=pl.CostEstimate(
             flops=4 * PACK * width * chunks * lanes,
@@ -132,7 +131,7 @@
             transcendentals=0,
         ),
         name="gram",
-    )(*map(near, (f, fp, cols, *before)))
+    )(*map(near, (f, fp, *cols, *before)))
 
 
 def place_kernel(orders, own_ref, other_ref, out_ref):
@@ -161,17 +160,22 @@
 
 def shards(n, inputs, out_grads, proj_in, proj_out, example_ids):
     bits = [1 << b for b in range(n.bit_length() - 2, 0, -1)]
-    orders = (bits, bits[:-2] + bits[-2:][::-1])
+    orders = (bits[:-2] + bits[-2:][::-1], bits[-1:] + bits[:-1])
     core = [(i, i ^ 1) for i in range(n)]
     f = features_of(inputs, out_grads, proj_in, proj_out, example_ids)
     fp = lax.ppermute(f, "row", core)
+
+    def swap(x, j):
+        return lax.ppermute(x, "row", [(i, i ^ orders[i & 1][j]) for i in range(n)])
+
+    last = len(bits) - 1
     held = f
-    for j in range(len(bits)):
-        perm = [(i, i ^ orders[i & 1][j]) for i in range(n)]
-        came = lax.ppermute(held, "row", perm)
-        if j < len(bits) - 1:
-            held = jnp.concatenate([held, came], axis=1)
-    own, other = gram_of(f, fp, came, gram_of(f, fp, held))
+    for j in range(last - 1):
+        held = jnp.concatenate([held, swap(held, j)], axis=1)
+    came = swap(held, last - 1)
+    first = swap(held, last)
+    second = swap(came, last)
+    own, other = gram_of(f, fp, [first, second], gram_of(f, fp, [held, came]))
     got = lax.ppermute(other, "row", core)
     return pl.pallas_call(
         functools.partial(place_kernel, orders),

time: 27.8 us -> 24.8 us (0.89)
  waiting for transfers between devices: 13.5 us -> 7.76 us
  starting transfers between devices: 6.77 us -> 9.54 us
    ppermute x3 -> x4, waiting for transfers between devices: 11.1 us -> 5.33 us  [swap(): return lax.ppermute(x, 'row', [(i, i ^ orders[i & 1][j]) for i in range(n)])]
    ppermute x3 -> x4, starting transfers between devices: 6.76 us -> 9.53 us  [swap(): return lax.ppermute(x, 'row', [(i, i ^ orders[i & 1][j]) for i in range(n)])]
  transfers between devices with their start and end apart: 5 -> 6, of which waited for: 5 -> 5; matrix products, arithmetic and copies ran while one was open for 0% -> 0% of each run, Pallas kernels for 1% -> 1%
where the time goes in v2:
time: 24.8 us; the launch traced here: 24.7 us
  starting transfers between devices  9.54 us (38%)
  waiting for transfers between devices  7.76 us (31%)
  Pallas kernels  7.32 us (30%)
    ppermute x4, starting transfers between devices, swap(): return lax.ppermute(x, 'row', [(i, i ^ orders[i & 1][j]) for i in range(n)])  9.53 us
    pallas_call x1, Pallas kernels, features_of(): pl.pallas_call(features_kernel, out_shape=pltpu.VMEM((rank * EX_DEV // 2...  5.91 us
    ppermute x4, waiting for transfers between devices, swap(): return lax.ppermute(x, 'row', [(i, i ^ orders[i & 1][j]) for i in range(n)])  5.33 us
    ppermute x1, waiting for transfers between devices, shards(): fp = lax.ppermute(f, 'row', core)  1.25 us
    ppermute x1, waiting for transfers between devices, shards(): got = lax.ppermute(other, 'row', core)  1.18 us
    pallas_call x1, Pallas kernels, shards(): pl.pallas_call(functools.partial(place_kernel, orders), out_shape=jax.Sha...  0.83 us
    pallas_call x2, Pallas kernels, gram_of(): pl.pallas_call(functools.partial(gram_kernel, len(cols)), out_shape=[pltp...  0.58 us
  transfers between devices with their start and end apart: 6, of which 5 were waited for; matrix products, arithmetic and copies ran while one was open for 0% of the time, Pallas kernels for 1%

profile of v2, /device:TPU:0, one launch (start us, length us, event | category | flops | bytes accessed | tf_op | source)
XLA Modules:
  0.0 24.7 jit_solution(14306156773018438802)
XLA Ops:
  0.0 5.9 %features.1.f_ref = bf16[16,16,128]{2,1,0:T(8,128)(2,1)S(1)} custom-call(s32[1,256]{1,0:T(1,128)} %bitcast.5, bf16[256,8192]{1,0:T(8,128)(2,1)} %x_hbm.1, bf16[256,8192]{1,0:T(8,128)(2,1)} %g_hbm.1, bf16[64,8192]{1,0:T(8,128)(2,1)} %bitcast.3, bf16[64,8192]{1,0:T(8,128)(2,1)} %bitcast.4), custom_call_target="tpu_custom_call" | custom-call | tf_op jit(solution)/shard_map/features/pallas_call | solution.py:75
  5.9 4.1 %collective-permute-start.1 = (bf16[16,16,128]{2,1,0:T(8,128)(2,1)S(1)}, bf16[16,16,128]{2,1,0:T(8,128)(2,1)S(1)}, u32[]{:S(2)}, u32[]{:S(2)}) collective-permute-start(bf16[16,16,128]{2,1,0:T(8,128)(2,1)S(1)} %features.1.f_ref), channel_id=1, source_target_pairs={{0,8},{1,3},{2,10},{3,1},{4,12},{5,7},{6,14},{7,5},{8,0},{9,11},{1... | collective-permute-start | bytes 196616 | tf_op jit(solution)/shard_map/ppermute | solution.py:169
  10.1 2.2 %collective-permute-done.1 = bf16[16,16,128]{2,1,0:T(8,128)(2,1)S(1)} collective-permute-done((bf16[16,16,128]{2,1,0:T(8,128)(2,1)S(1)}, bf16[16,16,128]{2,1,0:T(8,128)(2,1)S(1)}, u32[]{:S(2)}, u32[]{:S(2)}) %collective-permute-start.1) | collective-permute-done | bytes 65568 | tf_op jit(solution)/shard_map/ppermute | solution.py:169
  12.3 1.9 %collective-permute-start.3 = (bf16[16,32,128]{2,1,0:T(8,128)(2,1)S(1)}, bf16[16,32,128]{2,1,0:T(8,128)(2,1)S(1)}, u32[]{:S(2)}, u32[]{:S(2)}) collective-permute-start(bf16[16,32,128]{2,1,0:T(8,128)(2,1)S(1)} %pad_maximum_fusion.refs_0_), channel_id=1, source_target_pairs={{0,2},{1,9},{2,0},{3,11},{4,6},{5,13},{6,4},{7,15},{8,10},{9,1},{1... | collective-permute-start | bytes 393224 | tf_op jit(solution)/shard_map/ppermute | solution.py:169
  14.2 1.6 %collective-permute-start.2 = (bf16[16,32,128]{2,1,0:T(8,128)(2,1)S(1)}, bf16[16,32,128]{2,1,0:T(8,128)(2,1)S(1)}, u32[]{:S(2)}, u32[]{:S(2)}) collective-permute-start(bf16[16,32,128]{2,1,0:T(8,128)(2,1)S(1)} %pad_maximum_fusion.refs_0_), channel_id=1, source_target_pairs={{0,4},{1,5},{2,6},{3,7},{4,0},{5,1},{6,2},{7,3},{8,12},{9,13},{10,... | collective-permute-start | bytes 393224 | tf_op jit(solution)/shard_map/ppermute | solution.py:169
  15.8 1.5 %collective-permute-done.3.refs_1_ = bf16[16,32,128]{2,1,0:T(8,128)(2,1)S(1)} collective-permute-done((bf16[16,32,128]{2,1,0:T(8,128)(2,1)S(1)}, bf16[16,32,128]{2,1,0:T(8,128)(2,1)S(1)}, u32[]{:S(2)}, u32[]{:S(2)}) %collective-permute-start.3) | collective-permute-done | bytes 131104 | tf_op jit(solution)/shard_map/ppermute | solution.py:169
  17.3 1.9 %collective-permute-start.4 = (bf16[16,32,128]{2,1,0:T(8,128)(2,1)S(1)}, bf16[16,32,128]{2,1,0:T(8,128)(2,1)S(1)}, u32[]{:S(2)}, u32[]{:S(2)}) collective-permute-start(bf16[16,32,128]{2,1,0:T(8,128)(2,1)S(1)} %collective-permute-done.3.refs_1_), channel_id=1, source_target_pairs={{0,4},{1,5},{2,6},{3,7},{4,0},{5,1},{6,2},{7,3},{8,12},{9,13},{10,... | collective-permute-start | bytes 393224 | tf_op jit(solution)/shard_map/ppermute | solution.py:169
  19.2 0.0 collective-permute-start
  19.3 1.3 %collective-permute-done.fp_ref = bf16[16,16,128]{2,1,0:T(8,128)(2,1)S(1)} collective-permute-done((bf16[16,16,128]{2,1,0:T(8,128)(2,1)S(1)}, bf16[16,16,128]{2,1,0:T(8,128)(2,1)S(1)}, u32[]{:S(2)}, u32[]{:S(2)}) %collective-permute-start) | collective-permute-done | bytes 65568 | tf_op jit(solution)/shard_map/ppermute | solution.py:166
  20.5 0.3 %gram.2 = (f32[8,64]{1,0:T(8,128)S(1)}, f32[8,64]{1,0:T(8,128)S(1)}) custom-call(bf16[16,16,128]{2,1,0:T(8,128)(2,1)S(1)} %features.1.f_ref, bf16[16,16,128]{2,1,0:T(8,128)(2,1)S(1)} %collective-permute-done.fp_ref, bf16[16,32,128]{2,1,0:T(8,128)(2,1)S(1)} %pad_maximum_fusion.refs_0_, bf16[16,32,128]{2,1,0:T(8,128)(2,1)S(1)} %collective-permute-done.3.refs_1_), custom_call_target="tpu_custom_call" | custom-call | flops 8388608 | bytes 393216 | tf_op jit(solution)/shard_map/gram/pallas_call | solution.py:123
  20.8 0.0 collective-permute-done.2.refs_0_
  20.8 1.5 %collective-permute-done.4.refs_1_ = bf16[16,32,128]{2,1,0:T(8,128)(2,1)S(1)} collective-permute-done((bf16[16,32,128]{2,1,0:T(8,128)(2,1)S(1)}, bf16[16,32,128]{2,1,0:T(8,128)(2,1)S(1)}, u32[]{:S(2)}, u32[]{:S(2)}) %collective-permute-start.4) | collective-permute-done | bytes 131104 | tf_op jit(solution)/shard_map/ppermute | solution.py:169
  22.3 0.3 %gram.3 = (f32[8,128]{1,0:T(8,128)S(1)}, f32[8,128]{1,0:T(8,128)S(1)}) custom-call(bf16[16,16,128]{2,1,0:T(8,128)(2,1)S(1)} %features.1.f_ref, bf16[16,16,128]{2,1,0:T(8,128)(2,1)S(1)} %collective-permute-done.fp_ref, bf16[16,32,128]{2,1,0:T(8,128)(2,1)S(1)} %collective-permute-done.2.refs_0_, bf16[16,32,128]{2,1,0:T(8,128)(2,1)S(1)} %collective-permute-done.4.refs_1_, ...), custom_call_target="tpu_custom_call" | custom-call | flops 8388608 | bytes 393216 | tf_op jit(solution)/shard_map/gram/pallas_call | solution.py:123
  22.6 0.0 collective-permute-start.5
  22.6 1.2 %collective-permute-done.5.other_ref = f32[8,128]{1,0:T(8,128)S(1)} collective-permute-done((f32[8,128]{1,0:T(8,128)S(1)}, f32[8,128]{1,0:T(8,128)S(1)}, u32[]{:S(2)}, u32[]{:S(2)}) %collective-permute-start.5) | collective-permute-done | bytes 4128 | tf_op jit(solution)/shard_map/ppermute | solution.py:179
  23.8 0.8 %place.1 = f32[8,128]{1,0:T(8,128)} custom-call(f32[8,128]{1,0:T(8,128)S(1)} %get-tuple-element.11.own_ref, f32[8,128]{1,0:T(8,128)S(1)} %collective-permute-done.5.other_ref), custom_call_target="tpu_custom_call" | custom-call | tf_op jit(solution)/shard_map/place/pallas_call | solution.py:180
  (1 shorter events, 0.0 us)
Async XLA Ops:
  5.9 6.4 %collective-permute-start.1 = (bf16[16,16,128]{2,1,0:T(8,128)(2,1)S(1)}, bf16[16,16,128]{2,1,0:T(8,128)(2,1)S(1)}, u32[]{:S(2)}, u32[]{:S(2)}) collective-permute-start(bf16[16,16,128]{2,1,0:T(8,128)(2,1)S(1)} %features.1.f_ref), channel_id=1, source_target_pairs={{0,8},{1,3},{2,10},{3,1},{4,12},{5,7},{6,14},{7,5},{8,0},{9,11},{1... | collective-permute-start | bytes 196616 | tf_op jit(solution)/shard_map/ppermute | solution.py:169
  12.3 5.0 %collective-permute-start.3 = (bf16[16,32,128]{2,1,0:T(8,128)(2,1)S(1)}, bf16[16,32,128]{2,1,0:T(8,128)(2,1)S(1)}, u32[]{:S(2)}, u32[]{:S(2)}) collective-permute-start(bf16[16,32,128]{2,1,0:T(8,128)(2,1)S(1)} %pad_maximum_fusion.refs_0_), channel_id=1, source_target_pairs={{0,2},{1,9},{2,0},{3,11},{4,6},{5,13},{6,4},{7,15},{8,10},{9,1},{1... | collective-permute-start | bytes 393224 | tf_op jit(solution)/shard_map/ppermute | solution.py:169
  14.2 6.5 %collective-permute-start.2 = (bf16[16,32,128]{2,1,0:T(8,128)(2,1)S(1)}, bf16[16,32,128]{2,1,0:T(8,128)(2,1)S(1)}, u32[]{:S(2)}, u32[]{:S(2)}) collective-permute-start(bf16[16,32,128]{2,1,0:T(8,128)(2,1)S(1)} %pad_maximum_fusion.refs_0_), channel_id=1, source_target_pairs={{0,4},{1,5},{2,6},{3,7},{4,0},{5,1},{6,2},{7,3},{8,12},{9,13},{10,... | collective-permute-start | bytes 393224 | tf_op jit(solution)/shard_map/ppermute | solution.py:169
  17.3 5.0 %collective-permute-start.4 = (bf16[16,32,128]{2,1,0:T(8,128)(2,1)S(1)}, bf16[16,32,128]{2,1,0:T(8,128)(2,1)S(1)}, u32[]{:S(2)}, u32[]{:S(2)}) collective-permute-start(bf16[16,32,128]{2,1,0:T(8,128)(2,1)S(1)} %collective-permute-done.3.refs_1_), channel_id=1, source_target_pairs={{0,4},{1,5},{2,6},{3,7},{4,0},{5,1},{6,2},{7,3},{8,12},{9,13},{10,... | collective-permute-start | bytes 393224 | tf_op jit(solution)/shard_map/ppermute | solution.py:169
  19.2 1.3 %collective-permute-start = (bf16[16,16,128]{2,1,0:T(8,128)(2,1)S(1)}, bf16[16,16,128]{2,1,0:T(8,128)(2,1)S(1)}, u32[]{:S(2)}, u32[]{:S(2)}) collective-permute-start(bf16[16,16,128]{2,1,0:T(8,128)(2,1)S(1)} %features.1.f_ref), channel_id=1, source_target_pairs={{0,1},{1,0},{2,3},{3,2},{4,5},{5,4},{6,7},{7,6},{8,9},{9,8},{10,11... | collective-permute-start | bytes 196616 | tf_op jit(solution)/shard_map/ppermute | solution.py:166
  22.6 1.2 %collective-permute-start.5 = (f32[8,128]{1,0:T(8,128)S(1)}, f32[8,128]{1,0:T(8,128)S(1)}, u32[]{:S(2)}, u32[]{:S(2)}) collective-permute-start(f32[8,128]{1,0:T(8,128)S(1)} %get-tuple-element.12), channel_id=1, source_target_pairs={{0,1},{1,0},{2,3},{3,2},{4,5},{5,4},{6,7},{7,6},{8,9},{9,8},{10,11... | collective-permute-start | bytes 12296 | tf_op jit(solution)/shard_map/ppermute | solution.py:179
